TPU v7x, 256 devices: a whole 4x4x8 slice. The times are simulated.
256 devices in a mesh: blk: 16 (over z, x_lo), head: 4 (over x_hi, core), batch: 4 (over y).
Axes of the slice: x: 4 (x_hi: 2, x_lo: 2; x = x_hi * 2 + x_lo), y: 4, z: 8, core: 2. Of those that a mesh axis runs over, the one named last changes fastest.
Arguments:
- query_rows: bfloat16 [16384, 3072], P(('batch', 'blk'), 'head'), parts along dimension 0, may hold values from -6 to 6
- key_rows: bfloat16 [16384, 3072], P(('batch', 'blk'), 'head'), parts along dimension 0, may hold values from -6 to 6
- value_rows: bfloat16 [16384, 3072], P(('batch', 'blk'), 'head'), parts along dimension 0, may hold values from -6 to 6
- query_tangent: bfloat16 [16384, 3072], P(('batch', 'blk'), 'head'), parts along dimension 0, may hold values from -6 to 6
- key_tangent: bfloat16 [16384, 3072], P(('batch', 'blk'), 'head'), parts along dimension 0, may hold values from -6 to 6
- value_tangent: bfloat16 [16384, 3072], P(('batch', 'blk'), 'head'), parts along dimension 0, may hold values from -6 to 6
Outputs:
- attended: bfloat16 [16384, 3072], P(('batch', 'blk', 'head')), parts along dimension 0
- attended_tangent: bfloat16 [16384, 3072], P(('batch', 'blk', 'head')), parts along dimension 0
There are 4 independent parts, one for each index of `batch`. A program takes and returns all parts, laid end to end along the dimension named above; each array names one. Nothing has to cross between parts.
All inputs are finite; a program needn't handle non-finite values.
Results may differ from a plain program's by a relative error of at most 0.011.
Values may be sent and summed in bfloat16 or wider, within the bound.
A program may use at most 128 MiB of HBM per device.

v0:
```python
from functools import partial
import jax
import jax.numpy as jnp
from jax import lax
from jax.sharding import PartitionSpec as P

HD = 128
LOWEST = -1e30


def score_pair(query_heads, tangent_heads, key_block, key_change, scaling):
    scores = (
        jnp.einsum("qhd,khd->qhk", query_heads, key_block, preferred_element_type=jnp.float32)
        * scaling
    )
    score_change = (
        jnp.einsum("qhd,khd->qhk", tangent_heads, key_block, preferred_element_type=jnp.float32)
        + jnp.einsum("qhd,khd->qhk", query_heads, key_change, preferred_element_type=jnp.float32)
    ) * scaling
    return (scores, score_change)


def block_update(running, members, query_heads, tangent_heads, scaling):
    row_max, row_total, row_shift, numerator, tangent_numerator = running
    key_block, value_block, key_change, value_change = members
    scores, score_change = score_pair(query_heads, tangent_heads, key_block, key_change, scaling)
    new_max = jnp.maximum(row_max, jnp.max(scores, axis=2))
    shrink = jnp.exp(row_max - new_max)
    weights = jnp.exp(scores - new_max[:, :, None])
    mixed_terms = weights * score_change
    row_total = row_total * shrink + jnp.sum(weights, axis=2)
    row_shift = row_shift * shrink + jnp.sum(mixed_terms, axis=2)
    weights_low = weights.astype(jnp.bfloat16)
    mixed_low = mixed_terms.astype(jnp.bfloat16)
    numerator = numerator * shrink[:, :, None] + jnp.einsum(
        "qhk,khd->qhd", weights_low, value_block, preferred_element_type=jnp.float32
    )
    tangent_numerator = (
        tangent_numerator * shrink[:, :, None]
        + jnp.einsum("qhk,khd->qhd", mixed_low, value_block, preferred_element_type=jnp.float32)
        + jnp.einsum("qhk,khd->qhd", weights_low, value_change, preferred_element_type=jnp.float32)
    )
    return (new_max, row_total, row_shift, numerator, tangent_numerator)


def fold_keys(running, pieces, start, query_heads, tangent_heads):
    key_count = pieces[0].shape[0]
    head_count = query_heads.shape[1]
    head_width = query_heads.shape[2]
    block_rows = key_count
    while block_rows > 1024 and block_rows % 2 == 0:
        block_rows = block_rows // 2
    stacked = tuple(
        (
            member.reshape(key_count // block_rows, block_rows, head_count, head_width)
            for member in pieces
        )
    )
    scaling = head_width ** (-0.5)

    def advance(carried, members):
        return (block_update(carried, members, query_heads, tangent_heads, scaling), None)

    running, unused = lax.scan(advance, running, stacked)
    return running


def prepare(query_rows, query_tangent):
    query_heads = query_rows.reshape(query_rows.shape[0], -1, HD)
    tangent_heads = query_tangent.reshape(query_tangent.shape[0], -1, HD)
    rows_here = query_heads.shape[0]
    head_count = query_heads.shape[1]
    zero_stats = jnp.zeros((rows_here, head_count), jnp.float32)
    zero_rows = jnp.zeros((rows_here, head_count, HD), jnp.float32)
    initial = (
        jnp.full((rows_here, head_count), LOWEST, jnp.float32),
        zero_stats,
        zero_stats,
        zero_rows,
        zero_rows,
    )
    folder = partial(fold_keys, query_heads=query_heads, tangent_heads=tangent_heads)
    return (folder, initial)


def finish(running):
    row_max, row_total, row_shift, numerator, tangent_numerator = running
    attended = numerator / row_total[:, :, None]
    attended_tangent = (
        tangent_numerator / row_total[:, :, None] - (row_shift / row_total)[:, :, None] * attended
    )
    rows_here = attended.shape[0]
    return (
        attended.reshape(rows_here, -1).astype(jnp.bfloat16),
        attended_tangent.reshape(rows_here, -1).astype(jnp.bfloat16),
    )


def local(query_rows, key_rows, value_rows, query_tangent, key_tangent, value_tangent):
    folder, initial = prepare(query_rows, query_tangent)
    running = folder(
        initial,
        (
            lax.all_gather(key_rows, "blk", axis=0, tiled=True),
            lax.all_gather(value_rows, "blk", axis=0, tiled=True),
            lax.all_gather(key_tangent, "blk", axis=0, tiled=True),
            lax.all_gather(value_tangent, "blk", axis=0, tiled=True),
        ),
        jnp.int32(0),
    )
    result_rows, result_tangent = finish(running)
    attended, attended_tangent = (
        lax.all_to_all(result_rows, "head", split_axis=0, concat_axis=1, tiled=True),
        lax.all_to_all(result_tangent, "head", split_axis=0, concat_axis=1, tiled=True),
    )
    return (attended, attended_tangent)


def solution(mesh):
    return jax.shard_map(
        local,
        mesh=mesh,
        in_specs=(
            P(("batch", "blk"), "head"),
            P(("batch", "blk"), "head"),
            P(("batch", "blk"), "head"),
            P(("batch", "blk"), "head"),
            P(("batch", "blk"), "head"),
            P(("batch", "blk"), "head"),
        ),
        out_specs=(P(("batch", "blk", "head"), None), P(("batch", "blk", "head"), None)),
        check_vma=False,
    )
```

profile of v0, /device:TPU:1, one launch (start us, length us, event | category | flops | bytes accessed | tf_op | source)
XLA Modules:
  0.0 715.6 jit_solution(13581352506316343537)
XLA Ops:
  12.8 141.1 %all-gather.5.cloned.1.call-done = bf16[4096,768]{1,0:T(8,128)(2,1)} async-done(((bf16[256,768]{1,0:T(8,128)(2,1)}), bf16[4096,768]{1,0:T(8,128)(2,1)}) %all-gather.5.cloned.1.call-update) | async-done | bytes 6291472 | tf_op jit(solution)/shard_map/all_gather | solution.py:104
  153.9 13.7 %reshape.44 = bf16[4,1024,6,128]{3,2,1,0:T(8,128)(2,1)} reshape(bf16[4096,768]{1,0:T(8,128)(2,1)} %all-gather.5.cloned.1.call-done) | data formatting | bytes 12582912 | tf_op jit(solution)/shard_map/reshape | solution.py:55
  167.6 7.5 %copy.39 = bf16[4,1024,6,128]{3,1,2,0:T(8,128)(2,1)} copy(bf16[4,1024,6,128]{3,2,1,0:T(8,128)(2,1)} %reshape.44) | data formatting | bytes 12582912
  175.1 121.9 %all-gather.7.cloned.1.call-done = bf16[4096,768]{1,0:T(8,128)(2,1)} async-done(((bf16[256,768]{1,0:T(8,128)(2,1)}), bf16[4096,768]{1,0:T(8,128)(2,1)}) %all-gather.7.cloned.1.call-update) | async-done | bytes 6291472 | tf_op jit(solution)/shard_map/all_gather | solution.py:106
  297.0 13.7 %reshape.45 = bf16[4,1024,6,128]{3,2,1,0:T(8,128)(2,1)} reshape(bf16[4096,768]{1,0:T(8,128)(2,1)} %all-gather.7.cloned.1.call-done) | data formatting | bytes 12582912 | tf_op jit(solution)/shard_map/reshape | solution.py:55
  310.7 7.5 %copy.42 = bf16[4,1024,6,128]{3,1,2,0:T(8,128)(2,1)} copy(bf16[4,1024,6,128]{3,2,1,0:T(8,128)(2,1)} %reshape.45) | data formatting | bytes 12582912
  318.2 121.9 %all-gather.9.cloned.1.call-done = bf16[4096,768]{1,0:T(8,128)(2,1)} async-done(((bf16[256,768]{1,0:T(8,128)(2,1)}), bf16[4096,768]{1,0:T(8,128)(2,1)}) %all-gather.9.cloned.1.call-update) | async-done | bytes 6291472 | tf_op jit(solution)/shard_map/all_gather | solution.py:105
  440.1 13.7 %reshape.46 = bf16[4,1024,6,128]{3,2,1,0:T(8,128)(2,1)} reshape(bf16[4096,768]{1,0:T(8,128)(2,1)} %all-gather.9.cloned.1.call-done) | data formatting | bytes 12582912 | tf_op jit(solution)/shard_map/reshape | solution.py:55
  453.8 11.5 %copy.43 = bf16[4,1024,6,128]{1,3,2,0:T(8,128)(2,1)} copy(bf16[4,1024,6,128]{3,2,1,0:T(8,128)(2,1)} %reshape.46) | data formatting | bytes 12582912
  465.3 117.8 %all-gather.11.cloned.1.call-done = bf16[4096,768]{1,0:T(8,128)(2,1)} async-done(((bf16[256,768]{1,0:T(8,128)(2,1)}), bf16[4096,768]{1,0:T(8,128)(2,1)}) %all-gather.11.cloned.1.call-update) | async-done | bytes 6291472 | tf_op jit(solution)/shard_map/all_gather | solution.py:107
  583.0 13.7 %reshape.47 = bf16[4,1024,6,128]{3,2,1,0:T(8,128)(2,1)} reshape(bf16[4096,768]{1,0:T(8,128)(2,1)} %all-gather.11.cloned.1.call-done) | data formatting | bytes 12582912 | tf_op jit(solution)/shard_map/reshape | solution.py:55
  596.7 11.4 %copy.44 = bf16[4,1024,6,128]{1,3,2,0:T(8,128)(2,1)} copy(bf16[4,1024,6,128]{3,2,1,0:T(8,128)(2,1)} %reshape.47) | data formatting | bytes 12582912
  608.1 72.6 %while.19 = (s32[]{:T(128)}, f32[256,6]{0,1:T(8,128)S(1)}, f32[256,6]{0,1:T(8,128)S(1)}, f32[256,6]{0,1:T(8,128)S(1)}, f32[256,6,128]{0,2,1:T(8,128)S(1)}, /*ind...) while((s32[]{:T(128)}, f32[256,6]{0,1:T(8,128)S(1)}, ...), condition=%wide.region_4.5_spmd.clone, body=%wide.region_0.4_spmd.clone.sunk | while | flops 2445617664 | bytes 109863144 | solution.py:64
  608.1 5.0 bitcast_reduce_fusion.2
  626.3 5.1 bitcast_reduce_fusion.2
  634.6 4.0 fusion.91
  644.4 5.1 bitcast_reduce_fusion.2
  652.7 4.0 fusion.91
  662.6 5.1 bitcast_reduce_fusion.2
  670.9 4.0 fusion.91
  682.5 5.3 all-to-all-start
  689.4 6.5 all-to-all-done
  695.9 4.3 all-to-all-start.1
  701.0 7.3 %all-to-all-done.1 = bf16[4,64,768]{2,1,0:T(8,128)(2,1)S(1)} async-done(((bf16[4,64,768]{2,1,0:T(8,128)(2,1)}), bf16[4,64,768]{2,1,0:T(8,128)(2,1)S(1)}, u32[]{:S(2)}, u32[]{:S(2)}) %all-to-all-start.1) | async-done | bytes 393248 | tf_op jit(solution)/shard_map/all_to_all | solution.py:114
  (90 shorter events, 50.2 us)
Async XLA Ops:
  7.2 146.8 %all-gather.5.cloned.1.call-start = ((), (), s32[]{:S(2)}) async-start(), calls=%async_computation.2 | async-start | bytes 6684672 | tf_op jit(solution)/shard_map/all_gather | solution.py:104
  7.9 289.1 %all-gather.7.cloned.1.call-start = ((), (), s32[]{:S(2)}) async-start(), calls=%async_computation.3 | async-start | bytes 6684672 | tf_op jit(solution)/shard_map/all_gather | solution.py:106
  8.6 431.4 %all-gather.9.cloned.1.call-start = ((), (), s32[]{:S(2)}) async-start(), calls=%async_computation.4 | async-start | bytes 6684672 | tf_op jit(solution)/shard_map/all_gather | solution.py:105
  9.4 573.6 %all-gather.11.cloned.1.call-start = ((), (), s32[]{:S(2)}) async-start(), calls=%async_computation.5 | async-start | bytes 6684672 | tf_op jit(solution)/shard_map/all_gather | solution.py:107
  613.2 3.3 copy-start
  613.2 7.3 %slice-start = ((s8[6291456]{0:T(1024)(128)(4,1)}), s8[4194304]{0:T(1024)(128)(4,1)S(1)}, s32[]{:S(2)}) async-start(s8[6291456]{0:T(1024)(128)(4,1)} %bitcast.105), calls=%async_computation.6 | async-start | bytes 8388608 | tf_op jit(solution)/shard_map/while
  616.5 4.1 slice-start.1
  631.3 3.3 copy-start
  631.3 7.3 %slice-start = ((s8[6291456]{0:T(1024)(128)(4,1)}), s8[4194304]{0:T(1024)(128)(4,1)S(1)}, s32[]{:S(2)}) async-start(s8[6291456]{0:T(1024)(128)(4,1)} %bitcast.105), calls=%async_computation.6 | async-start | bytes 8388608 | tf_op jit(solution)/shard_map/while
  634.6 4.1 slice-start.1
  649.5 3.3 copy-start
  649.5 7.3 %slice-start = ((s8[6291456]{0:T(1024)(128)(4,1)}), s8[4194304]{0:T(1024)(128)(4,1)S(1)}, s32[]{:S(2)}) async-start(s8[6291456]{0:T(1024)(128)(4,1)} %bitcast.105), calls=%async_computation.6 | async-start | bytes 8388608 | tf_op jit(solution)/shard_map/while
  652.7 4.1 slice-start.1
  667.6 3.3 copy-start
  667.6 7.3 %slice-start = ((s8[6291456]{0:T(1024)(128)(4,1)}), s8[4194304]{0:T(1024)(128)(4,1)S(1)}, s32[]{:S(2)}) async-start(s8[6291456]{0:T(1024)(128)(4,1)} %bitcast.105), calls=%async_computation.6 | async-start | bytes 8388608 | tf_op jit(solution)/shard_map/while
  670.9 4.1 slice-start.1
  682.5 13.4 %all-to-all-start = ((bf16[4,64,768]{2,1,0:T(8,128)(2,1)}), bf16[4,64,768]{2,1,0:T(8,128)(2,1)S(1)}, u32[]{:S(2)}, u32[]{:S(2)}) async-start(bf16[4,64,768]{2,1,0:T(8,128)(2,1)} %convert_element_type.21), calls=%async_computation | async-start | bytes 786432 | tf_op jit(solution)/shard_map/all_to_all | solution.py:113
  695.9 12.4 %all-to-all-start.1 = ((bf16[4,64,768]{2,1,0:T(8,128)(2,1)}), bf16[4,64,768]{2,1,0:T(8,128)(2,1)S(1)}, u32[]{:S(2)}, u32[]{:S(2)}) async-start(bf16[4,64,768]{2,1,0:T(8,128)(2,1)} %convert_element_type.23), calls=%async_computation.1 | async-start | bytes 786432 | tf_op jit(solution)/shard_map/all_to_all | solution.py:114
Sparse Core Ops, SparseCore 0:
  9.8 144.0 all-gather.4
  155.7 141.2 all-gather.6
  298.8 141.2 all-gather.8
  441.7 141.2 all-gather.10
where the time goes:
time: 718 us; the launch traced here: 716 us
  waiting for transfers between devices  519 us (72%)
  local copies, waits for them, and re-layouts  103 us (14%)
  matrix products  65.1 us (9%)
  between operations  13.9 us (2%)
  starting transfers between devices  9.79 us (1%)
    all_gather x1, waiting for transfers between devices, local(): lax.all_gather(key_rows, 'blk', axis=0, tiled=True)  141 us
    all_gather x1, waiting for transfers between devices, local(): lax.all_gather(value_rows, 'blk', axis=0, tiled=True)  122 us
    all_gather x1, waiting for transfers between devices, local(): lax.all_gather(key_tangent, 'blk', axis=0, tiled=True)  122 us
    all_gather x1, waiting for transfers between devices, local(): lax.all_gather(value_tangent, 'blk', axis=0, tiled=True)  118 us
    reshape x4, local copies, waits for them, and re-layouts, fold_keys(): member.reshape(key_count // block_rows, block_rows, head_count, head_width)  54.7 us
    unnamed x8, local copies, waits for them, and re-layouts  40.7 us
    dot_general x4, matrix products, score_pair(): jnp.einsum('qhd,khd->qhk', query_heads, key_block, preferred_element_type...  20.2 us
    dot_general x4, matrix products, score_pair(): jnp.einsum('qhd,khd->qhk', query_heads, key_change, preferred_element_typ...  16.1 us
  transfers between devices with their start and end apart: 6, of which 6 were waited for; matrix products, arithmetic and copies ran while one was open for 10% of the time, Pallas kernels for 0%

commit v1 on v0

--- a/solution.py
+++ b/solution.py
@@ -1,11 +1,25 @@
+import functools
 from functools import partial
 import jax
 import jax.numpy as jnp
 from jax import lax
 from jax.sharding import PartitionSpec as P
+from jax.lax import all_to_all, axis_size
 
 HD = 128
 LOWEST = -1e30
+
+
+def drive_the_matrix(array_here, axis_id):
+    crops = []
+    for _ in range(axis_size(axis_id)):
+        crops.append(array_here)
+    carry_in = all_to_all(jnp.stack(crops), axis_name=axis_id, split_axis=0, concat_axis=0)
+    v1 = jnp.concatenate(carry_in, 0)
+    return v1
+
+
+point_series_all = functools.partial(drive_the_matrix, axis_id="blk")
 
 
 def score_pair(query_heads, tangent_heads, key_block, key_change, scaling):
@@ -104,7 +118,7 @@
             lax.all_gather(key_rows, "blk", axis=0, tiled=True),
             lax.all_gather(value_rows, "blk", axis=0, tiled=True),
             lax.all_gather(key_tangent, "blk", axis=0, tiled=True),
-            lax.all_gather(value_tangent, "blk", axis=0, tiled=True),
+            point_series_all(value_tangent),
         ),
         jnp.int32(0),
     )

time: 718 us -> 678 us (0.944)
  waiting for transfers between devices: 519 us -> 465 us
  starting transfers between devices: 9.79 us -> 20 us
    all_to_all x0 -> x1, waiting for transfers between devices: none -> 176 us  [drive_the_matrix(): all_to_all(jnp.stack(crops), axis_name=axis_id, split_axis=0, concat_axis=0)]
    all_gather x1 -> x0, waiting for transfers between devices: 118 us -> none  [local(): lax.all_gather(value_tangent, 'blk', axis=0, tiled=True)]
    all_gather x1, waiting for transfers between devices: 141 us -> 30.9 us  [local(): lax.all_gather(key_rows, 'blk', axis=0, tiled=True)]
    another operation x0 -> x2, local copies, waits for them, and re-layouts: none -> 13.5 us  [the longest x1 10.2 us: fold_keys(): member.reshape(key_count // block_rows, block_rows, head_count, head_width)]
    reshape x4 -> x3, local copies, waits for them, and re-layouts: 54.7 us -> 41.3 us  [fold_keys(): member.reshape(key_count // block_rows, block_rows, head_count, head_width)]
    all_to_all x0 -> x1, starting transfers between devices: none -> 10.2 us  [drive_the_matrix(): all_to_all(jnp.stack(crops), axis_name=axis_id, split_axis=0, concat_axis=0)]
    all_to_all x0 -> x1, local copies, waits for them, and re-layouts: none -> 9.07 us  [drive_the_matrix(): all_to_all(jnp.stack(crops), axis_name=axis_id, split_axis=0, concat_axis=0)]
    unnamed x8 -> x13, local copies, waits for them, and re-layouts: 40.7 us -> 35.7 us
  transfers between devices with their start and end apart: 6 -> 6, of which waited for: 6 -> 6; matrix products, arithmetic and copies ran while one was open for 10% -> 11% of each run, Pallas kernels for 0% -> 0%
where the time goes in v1:
time: 678 us; the launch traced here: 676 us
  waiting for transfers between devices  465 us (69%)
  local copies, waits for them, and re-layouts  107 us (16%)
  matrix products  65.2 us (10%)
  starting transfers between devices  20 us (3%)
  between operations  13.9 us (2%)
    all_to_all x1, waiting for transfers between devices, drive_the_matrix(): all_to_all(jnp.stack(crops), axis_name=axis_id, split_axis=0, concat_axis=0)  176 us
    all_gather x1, waiting for transfers between devices, local(): lax.all_gather(value_rows, 'blk', axis=0, tiled=True)  122 us
    all_gather x1, waiting for transfers between devices, local(): lax.all_gather(key_tangent, 'blk', axis=0, tiled=True)  120 us
    reshape x3, local copies, waits for them, and re-layouts, fold_keys(): member.reshape(key_count // block_rows, block_rows, head_count, head_width)  41.3 us
    unnamed x13, local copies, waits for them, and re-layouts  35.7 us
    all_gather x1, waiting for transfers between devices, local(): lax.all_gather(key_rows, 'blk', axis=0, tiled=True)  30.9 us
    dot_general x4, matrix products, score_pair(): jnp.einsum('qhd,khd->qhk', query_heads, key_block, preferred_element_type...  20.4 us
    dot_general x4, matrix products, score_pair(): jnp.einsum('qhd,khd->qhk', query_heads, key_change, preferred_element_typ...  16.1 us
  transfers between devices with their start and end apart: 6, of which 6 were waited for; matrix products, arithmetic and copies ran while one was open for 11% of the time, Pallas kernels for 0%

profile of v1, /device:TPU:1, one launch (start us, length us, event | category | flops | bytes accessed | tf_op | source)
XLA Modules:
  0.0 675.8 jit_solution(4746782658757693137)
XLA Ops:
  13.1 10.2 %all-to-all-start = ((bf16[16,256,768]{1,2,0:T(8,128)(2,1)}), bf16[16,256,768]{1,2,0:T(8,128)(2,1)}, u32[]{:S(2)}, u32[]{:S(2)}) async-start(bf16[16,256,768]{1,2,0:T(8,128)(2,1)} %stack.2), calls=%async_computation | async-start | bytes 12582912 | tf_op jit(solution)/shard_map/all_to_all | solution.py:17
  25.0 176.0 %all-to-all-done = bf16[16,256,768]{1,2,0:T(8,128)(2,1)} async-done(((bf16[16,256,768]{1,2,0:T(8,128)(2,1)}), bf16[16,256,768]{1,2,0:T(8,128)(2,1)}, u32[]{:S(2)}, u32[]{:S(2)}) %all-to-all-start) | async-done | bytes 6291488 | tf_op jit(solution)/shard_map/all_to_all | solution.py:17
  201.0 9.1 %copy.58 = bf16[16,256,768]{1,0,2:T(8,128)(2,1)} copy(bf16[16,256,768]{1,2,0:T(8,128)(2,1)} %all-to-all-done) | data formatting | bytes 12582912 | tf_op jit(solution)/shard_map/all_to_all | solution.py:17
  210.1 10.2 %reshape_reshape.3 = bf16[4,1024,6,128]{1,0,3,2:T(4,128)(2,1)} reshape(bf16[16,256,768]{1,0,2:T(8,128)(2,1)} %copy.58) | data formatting | bytes 12582912 | tf_op jit(solution)/shard_map/reshape;reshape | solution.py:69
  220.2 7.5 %copy.64 = bf16[4,1024,6,128]{1,3,2,0:T(8,128)(2,1)} copy(bf16[4,1024,6,128]{1,0,3,2:T(4,128)(2,1)} %reshape_reshape.3) | data formatting | bytes 12582912
  227.7 30.9 %all-gather.4.cloned.1.call-done = bf16[4096,768]{1,0:T(8,128)(2,1)} async-done(((bf16[256,768]{1,0:T(8,128)(2,1)}), bf16[4096,768]{1,0:T(8,128)(2,1)}) %all-gather.4.cloned.1.call-update) | async-done | bytes 6291472 | tf_op jit(solution)/shard_map/all_gather | solution.py:118
  258.6 13.8 %reshape.42 = bf16[4,1024,6,128]{3,2,1,0:T(8,128)(2,1)} reshape(bf16[4096,768]{1,0:T(8,128)(2,1)} %all-gather.4.cloned.1.call-done) | data formatting | bytes 12582912 | tf_op jit(solution)/shard_map/reshape | solution.py:69
  272.4 7.4 %copy.59 = bf16[4,1024,6,128]{3,1,2,0:T(8,128)(2,1)} copy(bf16[4,1024,6,128]{3,2,1,0:T(8,128)(2,1)} %reshape.42) | data formatting | bytes 12582912
  279.8 120.2 %all-gather.6.cloned.1.call-done = bf16[4096,768]{1,0:T(8,128)(2,1)} async-done(((bf16[256,768]{1,0:T(8,128)(2,1)}), bf16[4096,768]{1,0:T(8,128)(2,1)}) %all-gather.6.cloned.1.call-update) | async-done | bytes 6291472 | tf_op jit(solution)/shard_map/all_gather | solution.py:120
  400.0 13.8 %reshape.43 = bf16[4,1024,6,128]{3,2,1,0:T(8,128)(2,1)} reshape(bf16[4096,768]{1,0:T(8,128)(2,1)} %all-gather.6.cloned.1.call-done) | data formatting | bytes 12582912 | tf_op jit(solution)/shard_map/reshape | solution.py:69
  413.7 7.4 %copy.62 = bf16[4,1024,6,128]{3,1,2,0:T(8,128)(2,1)} copy(bf16[4,1024,6,128]{3,2,1,0:T(8,128)(2,1)} %reshape.43) | data formatting | bytes 12582912
  421.1 121.9 %all-gather.8.cloned.1.call-done = bf16[4096,768]{1,0:T(8,128)(2,1)} async-done(((bf16[256,768]{1,0:T(8,128)(2,1)}), bf16[4096,768]{1,0:T(8,128)(2,1)}) %all-gather.8.cloned.1.call-update) | async-done | bytes 6291472 | tf_op jit(solution)/shard_map/all_gather | solution.py:119
  543.0 13.8 %reshape.44 = bf16[4,1024,6,128]{3,2,1,0:T(8,128)(2,1)} reshape(bf16[4096,768]{1,0:T(8,128)(2,1)} %all-gather.8.cloned.1.call-done) | data formatting | bytes 12582912 | tf_op jit(solution)/shard_map/reshape | solution.py:69
  556.8 11.5 %copy.63 = bf16[4,1024,6,128]{1,3,2,0:T(8,128)(2,1)} copy(bf16[4,1024,6,128]{3,2,1,0:T(8,128)(2,1)} %reshape.44) | data formatting | bytes 12582912
  568.2 72.7 %while.19 = (s32[]{:T(128)}, f32[256,6]{0,1:T(8,128)S(1)}, f32[256,6]{0,1:T(8,128)S(1)}, f32[256,6]{0,1:T(8,128)S(1)}, f32[256,6,128]{0,2,1:T(8,128)S(1)}, /*ind...) while((s32[]{:T(128)}, f32[256,6]{0,1:T(8,128)S(1)}, ...), condition=%wide.region_4.5_spmd.clone, body=%wide.region_0.4_spmd.clone.sunk | while | flops 2445617664 | bytes 109863144 | solution.py:78
  568.2 5.1 bitcast_reduce_fusion.2
  576.6 4.0 fusion.91
  586.4 5.1 bitcast_reduce_fusion.2
  604.6 5.1 bitcast_reduce_fusion.2
  622.8 5.1 bitcast_reduce_fusion.2
  642.7 5.3 all-to-all-start.1
  649.6 6.5 all-to-all-done.1
  656.2 4.3 all-to-all-start.2
  661.2 7.3 %all-to-all-done.2 = bf16[4,64,768]{2,1,0:T(8,128)(2,1)S(1)} async-done(((bf16[4,64,768]{2,1,0:T(8,128)(2,1)}), bf16[4,64,768]{2,1,0:T(8,128)(2,1)S(1)}, u32[]{:S(2)}, u32[]{:S(2)}) %all-to-all-start.2) | async-done | bytes 393248 | tf_op jit(solution)/shard_map/all_to_all | solution.py:128
  (96 shorter events, 60.1 us)
Async XLA Ops:
  7.2 251.5 %all-gather.4.cloned.1.call-start = ((), (), s32[]{:S(2)}) async-start(), calls=%async_computation.3 | async-start | bytes 6684672 | tf_op jit(solution)/shard_map/all_gather | solution.py:118
  7.9 392.1 %all-gather.6.cloned.1.call-start = ((), (), s32[]{:S(2)}) async-start(), calls=%async_computation.4 | async-start | bytes 6684672 | tf_op jit(solution)/shard_map/all_gather | solution.py:120
  13.1 11.0 %copy-start.1 = (bf16[256,768]{1,0:T(8,128)(2,1)S(1)}, bf16[256,768]{1,0:T(8,128)(2,1)}, u32[]{:S(2)}) copy-start(bf16[256,768]{1,0:T(8,128)(2,1)} %param.8) | copy-start | bytes 1179652
  13.1 11.4 %copy-start.2 = (bf16[256,768]{1,0:T(8,128)(2,1)S(1)}, bf16[256,768]{1,0:T(8,128)(2,1)}, u32[]{:S(2)}) copy-start(bf16[256,768]{1,0:T(8,128)(2,1)} %param.11) | copy-start | bytes 1179652
  13.1 187.8 %all-to-all-start = ((bf16[16,256,768]{1,2,0:T(8,128)(2,1)}), bf16[16,256,768]{1,2,0:T(8,128)(2,1)}, u32[]{:S(2)}, u32[]{:S(2)}) async-start(bf16[16,256,768]{1,2,0:T(8,128)(2,1)} %stack.2), calls=%async_computation | async-start | bytes 12582912 | tf_op jit(solution)/shard_map/all_to_all | solution.py:17
  23.4 519.7 %all-gather.8.cloned.1.call-start = ((), (), s32[]{:S(2)}) async-start(), calls=%async_computation.5 | async-start | bytes 6684672 | tf_op jit(solution)/shard_map/all_gather | solution.py:119
  573.3 3.3 copy-start
  573.4 7.3 %slice-start = ((s8[6291456]{0:T(1024)(128)(4,1)}), s8[4194304]{0:T(1024)(128)(4,1)S(1)}, s32[]{:S(2)}) async-start(s8[6291456]{0:T(1024)(128)(4,1)} %bitcast.107), calls=%async_computation.6 | async-start | bytes 8388608 | tf_op jit(solution)/shard_map/while
  576.6 4.1 slice-start.1
  591.5 3.3 copy-start
  591.5 7.3 %slice-start = ((s8[6291456]{0:T(1024)(128)(4,1)}), s8[4194304]{0:T(1024)(128)(4,1)S(1)}, s32[]{:S(2)}) async-start(s8[6291456]{0:T(1024)(128)(4,1)} %bitcast.107), calls=%async_computation.6 | async-start | bytes 8388608 | tf_op jit(solution)/shard_map/while
  594.8 4.1 slice-start.1
  609.7 3.3 copy-start
  609.7 7.3 %slice-start = ((s8[6291456]{0:T(1024)(128)(4,1)}), s8[4194304]{0:T(1024)(128)(4,1)S(1)}, s32[]{:S(2)}) async-start(s8[6291456]{0:T(1024)(128)(4,1)} %bitcast.107), calls=%async_computation.6 | async-start | bytes 8388608 | tf_op jit(solution)/shard_map/while
  613.0 4.1 slice-start.1
  627.9 3.3 copy-start
  627.9 7.3 %slice-start = ((s8[6291456]{0:T(1024)(128)(4,1)}), s8[4194304]{0:T(1024)(128)(4,1)S(1)}, s32[]{:S(2)}) async-start(s8[6291456]{0:T(1024)(128)(4,1)} %bitcast.107), calls=%async_computation.6 | async-start | bytes 8388608 | tf_op jit(solution)/shard_map/while
  631.2 4.1 slice-start.1
  642.7 13.4 %all-to-all-start.1 = ((bf16[4,64,768]{2,1,0:T(8,128)(2,1)}), bf16[4,64,768]{2,1,0:T(8,128)(2,1)S(1)}, u32[]{:S(2)}, u32[]{:S(2)}) async-start(bf16[4,64,768]{2,1,0:T(8,128)(2,1)} %convert_element_type.21), calls=%async_computation.1 | async-start | bytes 786432 | tf_op jit(solution)/shard_map/all_to_all | solution.py:127
  656.2 12.4 %all-to-all-start.2 = ((bf16[4,64,768]{2,1,0:T(8,128)(2,1)}), bf16[4,64,768]{2,1,0:T(8,128)(2,1)S(1)}, u32[]{:S(2)}, u32[]{:S(2)}) async-start(bf16[4,64,768]{2,1,0:T(8,128)(2,1)} %convert_element_type.23), calls=%async_computation.2 | async-start | bytes 786432 | tf_op jit(solution)/shard_map/all_to_all | solution.py:128
Sparse Core Ops, SparseCore 0:
  9.8 248.8 all-gather.3
  260.4 139.4 all-gather.5
  401.7 141.2 all-gather.7
